TPU v7x, 32 devices: a whole 2x2x4 slice. The times are simulated.
32 devices in a mesh: shot: 4 (over z), tile: 8 (over y, x, core).
Axes of the slice: x: 2, y: 2, z: 4, core: 2. Of those that a mesh axis runs over, the one named last changes fastest.
Arguments:
- traces: bfloat16 [2, 4, 1024, 2048], P(None, 'shot', 'tile'), may hold values from -6 to 6
- start: int32 [4, 8, 8], P('shot'), may hold values from 0 to 1536
- depth_index: int32 [4, 8, 8, 256], P('shot', 'tile'), may hold values from 0 to 510
- depth_frac: bfloat16 [4, 8, 8, 256], P('shot', 'tile'), may hold values from 0 to 1
- aperture: int32 [4, 8, 4], P('shot'), may hold values from -1 to 7, as said below
- amplitude: bfloat16 [4, 8, 8, 384, 128], P('shot', 'tile'), may hold values from -0.5 to 0.5
Outputs:
- migrated: float32 [3072, 256], P('tile', 'shot')
Inputs may be any that keep to these rules, and one draw needn't show every extreme that they name: `aperture`: each list holds 1 to 4 block ids, ascending and consecutive, then -1 in the remaining slots; in every shot some tile's list is full.
All inputs are finite; a program needn't handle non-finite values.
Results may differ from a plain program's by a relative error of at most 0.0041.
Values may be sent and summed in bfloat16 or wider, within the bound.
No kernel may reach another device: no remote copies, remote signals or barrier semaphores. Data moves between devices by JAX's collectives and lax.ppermute only.
A program may use at most 64 MiB of HBM per device.

v0:
```python
import functools

import jax
import jax.numpy as jnp
from jax import lax
from jax.experimental import pallas as pl
from jax.experimental.pallas import tpu as pltpu
from jax.sharding import PartitionSpec as P

TW = 512
LANES = 128
SLAB = TW + LANES
NT_DIMS = (((1,), (1,)), ((), ()))
VMEM = pl.BlockSpec(memory_space=pltpu.VMEM)
HBM = pl.BlockSpec(memory_space=pltpu.HBM)


def target_of(pos, step, count):
    if count & (count - 1) == 0:
        return pos ^ step
    return (pos + step) % count


def source_of(pos, step, count):
    if count & (count - 1) == 0:
        return pos ^ step
    return (pos - step + count) % count


def pairs(step, count):
    return [(pos, target_of(pos, step, count)) for pos in range(count)]


def chip_pairs(step, tiles):
    return [
        (pos, 2 * target_of(pos // 2, step, tiles // 2) + pos % 2) for pos in range(tiles)
    ]


def steps_of(count):
    return list(range(count // 2, count)) + list(range(1, count // 2))


def near_first(count):
    return sorted(range(1, count), key=lambda step: (step.bit_count(), step))


def chip_of(step, tiles):
    me = lax.axis_index("tile")
    if step == 0:
        return me, me
    chips = tiles // 2
    served = 2 * target_of(me // 2, step, chips) + me % 2
    return served, 2 * source_of(me // 2, step, chips) + me % 2


def wanted_kernel(tiles, index_hbm, frac_hbm, start_hbm, aperture_hbm, traces_hbm, *refs):
    traces_ref, codes_ref, *out_refs, index_ref, frac_ref, start_ref, aperture_ref, sems = refs
    copies = [
        pltpu.make_async_copy(source, target, sems.at[place])
        for place, (source, target) in enumerate(
            [
                (index_hbm, index_ref),
                (frac_hbm, frac_ref),
                (start_hbm, start_ref),
                (aperture_hbm, aperture_ref),
                (traces_hbm, traces_ref),
            ]
        )
    ]
    for copy in copies:
        copy.start()
    for copy in copies[:4]:
        copy.wait()
    me = lax.axis_index("tile")
    rows = index_ref[...].astype(jnp.float32)
    weights = frac_ref[...].astype(jnp.float32)
    starts = start_ref[...]
    slots = aperture_ref[...]
    position = lax.broadcasted_iota(jnp.int32, rows.shape, 0)
    start_tile = lax.broadcasted_iota(jnp.int32, starts.shape, 0)
    start_block = lax.broadcasted_iota(jnp.int32, starts.shape, 1)
    slot_tile = lax.broadcasted_iota(jnp.int32, slots.shape, 1)
    for step, out_ref in enumerate(out_refs):
        tile, block = chip_of(step, tiles)
        for other in range(2):
            mine = position == (block ^ other)
            out_ref[other : other + 1] = jnp.sum(
                jnp.where(mine, rows, 0.0), axis=0, keepdims=True
            )
            out_ref[2 + other : 3 + other] = jnp.sum(
                jnp.where(mine, weights, 0.0), axis=0, keepdims=True
            )
            here = jnp.logical_and(start_tile == tile, start_block == (me ^ other))
            first = jnp.where(here, starts, 0).astype(jnp.float32)
            first = jnp.sum(jnp.sum(first, axis=1, keepdims=True), axis=0, keepdims=True)
            hits = jnp.logical_and(slot_tile == tile, slots == (me ^ other))
            hits = jnp.where(hits, 1.0, 0.0)
            hits = jnp.max(jnp.max(hits, axis=1, keepdims=True), axis=0, keepdims=True)
            code = jnp.where(hits > 0.0, first, -1.0).astype(jnp.int32)
            place = 2 * step + other
            codes_ref[place : place + 1] = jnp.broadcast_to(code, (1, codes_ref.shape[1]))
    copies[4].wait()


def interpolate(columns, other, shift, window):
    row = columns[:, other : other + 1] + shift
    weight = columns[:, 2 + other : 3 + other]
    depth = row.shape[0]
    lane = lax.broadcasted_iota(jnp.int32, (depth, window.shape[1]), 1).astype(jnp.float32)
    hot = jnp.concatenate(
        [(lane == row).astype(jnp.bfloat16), (lane == row + 1.0).astype(jnp.bfloat16)], axis=0
    )
    both = lax.dot_general(hot, window, NT_DIMS, preferred_element_type=jnp.float32)
    return ((1.0 - weight) * both[:depth] + weight * both[depth:]).astype(jnp.bfloat16)


def depth_kernel(step, codes_ref, own_ref, other_ref, wanted_ref, out_ref):
    last = own_ref.shape[2] // LANES - SLAB // LANES
    columns = wanted_ref[...].T
    for other, traces_ref in enumerate((own_ref, other_ref)):
        first = codes_ref[2 * step + other, 0]

        @pl.when(first >= 0)
        def _():
            slab = pl.multiple_of(jnp.minimum(first // LANES, last) * LANES, LANES)
            window = jnp.concatenate(
                [traces_ref[0, :, pl.ds(slab, SLAB)], traces_ref[1, :, pl.ds(slab, SLAB)]], axis=0
            )
            shift = (first - slab).astype(jnp.float32)
            out_ref[other] = interpolate(columns, other, shift, window)

        @pl.when(first < 0)
        def _():
            out_ref[other] = jnp.zeros(out_ref.shape[1:], out_ref.dtype)


def add_chips(tiles, steps, amplitude_ref, depth_refs, total_ref, fresh):
    receivers = amplitude_ref.shape[2]
    group = 4
    for base in range(0, len(steps), group):
        places = range(base, min(base + group, len(steps)))
        weights = []
        for place in places:
            _, block = chip_of(steps[place], tiles)
            weights += [amplitude_ref[block], amplitude_ref[block ^ 1]]
        weights = jnp.concatenate(weights, axis=1)
        for part in range(2):
            lanes = slice(part * receivers, (part + 1) * receivers)
            traces = jnp.concatenate(
                [depth_refs[place][other, :, lanes] for place in places for other in range(2)],
                axis=1,
            )
            added = lax.dot_general(traces, weights, NT_DIMS, preferred_element_type=jnp.float32)
            if base or not fresh:
                added = added + total_ref[part]
            total_ref[part] = added


def gather_kernel(tiles, steps, amplitude_ref, *refs):
    add_chips(tiles, steps, amplitude_ref, refs[:-1], refs[-1], True)


def partial_kernel(tiles, shots, steps, amplitude_ref, before_ref, *refs):
    my_shot = lax.axis_index("shot")
    depth_refs = refs[: len(steps)]
    own_ref, out_refs, total_ref = refs[len(steps)], refs[len(steps) + 1 : -1], refs[-1]
    span = own_ref.shape[1]
    total_ref[...] = before_ref[...]
    add_chips(tiles, steps, amplitude_ref, depth_refs, total_ref, False)
    for part in range(2):
        own_ref[part] = total_ref[part, pl.ds(pl.multiple_of(my_shot * span, span), span), :]
        for place, step in enumerate(steps_of(shots)):
            target = target_of(my_shot, step, shots)
            rows = pl.ds(pl.multiple_of(target * span, span), span)
            out_refs[place][part] = total_ref[part, rows, :].astype(jnp.bfloat16)


def add_shots(refs, sums):
    stack, first, second = sums
    for ref in refs:
        real = ref[0].astype(jnp.float32)
        imag = ref[1].astype(jnp.float32)
        inverse = 1.0 / jnp.maximum(jnp.sqrt(real * real + imag * imag), 1.0)
        stack, first, second = stack + real, first + real * inverse, second + imag * inverse
    return stack, first, second


def early_kernel(*refs):
    zero = jnp.zeros(refs[0].shape[1:], jnp.float32)
    sums = add_shots(refs[:-1], (zero, zero, zero))
    for place, value in enumerate(sums):
        refs[-1][place] = value


def image_kernel(shots, sums_ref, *refs):
    stack, first, second = add_shots(refs[:-1], (sums_ref[0], sums_ref[1], sums_ref[2]))
    refs[-1][...] = stack * (first * first + second * second) / (shots * shots)


def local(traces, start, depth_index, depth_frac, aperture, amplitude):
    tiles = lax.axis_size("tile")
    shots = lax.axis_size("shot")
    parts, _, receivers, samples = traces.shape
    depth = depth_index.shape[3]
    columns = amplitude.shape[3]
    piece = depth // shots
    chips = tiles // 2
    away = near_first(chips)
    params = pltpu.CompilerParams(vmem_limit_bytes=32 << 20)
    small = pltpu.CompilerParams(vmem_limit_bytes=8 << 20)

    other_traces = lax.ppermute(traces[:, 0], "tile", [(pos, pos ^ 1) for pos in range(tiles)])

    inputs = [depth_index[0, 0], depth_frac[0, 0], start[0], aperture[0].T, traces[:, 0]]
    own_traces, codes, *wanted = pl.pallas_call(
        functools.partial(wanted_kernel, tiles),
        out_shape=[
            jax.ShapeDtypeStruct((parts, receivers, samples), traces.dtype),
            jax.ShapeDtypeStruct((tiles, LANES), jnp.int32),
        ]
        + [jax.ShapeDtypeStruct((4, depth), jnp.float32)] * chips,
        in_specs=[HBM] * len(inputs),
        out_specs=[VMEM] * (2 + chips),
        scratch_shapes=[pltpu.VMEM(value.shape, value.dtype) for value in inputs[:-1]]
        + [pltpu.SemaphoreType.DMA((len(inputs),))],
        compiler_params=params,
    )(*[pltpu.with_memory_space_constraint(value, pltpu.HBM) for value in inputs])
    asked = {
        step: lax.ppermute(wanted[step], "tile", chip_pairs(step, tiles))
        for step in away
    }

    def depth_traces(step, request):
        return pl.pallas_call(
            functools.partial(depth_kernel, step),
            out_shape=jax.ShapeDtypeStruct((2, depth, parts * receivers), jnp.bfloat16),
            in_specs=[VMEM] * 4,
            out_specs=VMEM,
            compiler_params=params,
            cost_estimate=pl.CostEstimate(
                flops=8 * depth * SLAB * parts * receivers,
                bytes_accessed=8 * parts * receivers * (samples + depth),
                transcendentals=0,
            ),
        )(codes, own_traces, other_traces, request)

    kept = depth_traces(0, wanted[0])
    received = [kept]
    for step in away:
        request = asked[step]
        sent = depth_traces(step, request)
        received.append(lax.ppermute(sent, "tile", chip_pairs(step, tiles)))

    own = jax.ShapeDtypeStruct((parts, piece, columns), jnp.float32)
    other = jax.ShapeDtypeStruct((parts, piece, columns), jnp.bfloat16)
    steps = [0] + away
    early = (chips + 1) // 2
    total = jax.ShapeDtypeStruct((parts, depth, columns), jnp.float32)
    before = pl.pallas_call(
        functools.partial(gather_kernel, tiles, steps[:early]),
        out_shape=total,
        in_specs=[VMEM] * (1 + early),
        out_specs=VMEM,
        compiler_params=params,
    )(amplitude[0, 0], *received[:early])
    pieces = pl.pallas_call(
        functools.partial(partial_kernel, tiles, shots, steps[early:]),
        out_shape=[own] + [other] * (shots - 1),
        in_specs=[VMEM] * (2 + chips - early),
        out_specs=[VMEM] * shots,
        scratch_shapes=[pltpu.VMEM(total.shape, total.dtype)],
        compiler_params=params,
    )(amplitude[0, 0], before, *received[early:])
    summed = [pieces[0]]
    for place, step in enumerate(steps_of(shots)):
        summed.append(lax.ppermute(pieces[1 + place], "shot", pairs(step, shots)))

    early = 2
    sums = pl.pallas_call(
        early_kernel,
        out_shape=jax.ShapeDtypeStruct((3, piece, columns), jnp.float32),
        in_specs=[VMEM] * early,
        out_specs=VMEM,
        compiler_params=params,
    )(*summed[:early])
    image = pl.pallas_call(
        functools.partial(image_kernel, shots),
        out_shape=jax.ShapeDtypeStruct((piece, columns), jnp.float32),
        in_specs=[VMEM] * (1 + shots - early),
        out_specs=VMEM,
        compiler_params=small,
    )(sums, *summed[early:])
    return image.T


def solution(mesh):
    in_specs = (
        P(None, "shot", "tile", None),
        P("shot", None, None),
        P("shot", "tile", None, None),
        P("shot", "tile", None, None),
        P("shot", None, None),
        P("shot", "tile", None, None, None),
    )
    out_specs = P("tile", "shot")
    return jax.shard_map(local, mesh=mesh, in_specs=in_specs, out_specs=out_specs, check_vma=False)
```

profile of v0, /device:TPU:0, one launch (start us, length us, event | category | flops | bytes accessed | tf_op | source)
XLA Modules:
  0.0 34.6 jit_solution(14624761995188522197)
XLA Ops:
  0.0 0.5 %collective-permute-start = (bf16[2,128,2048]{2,1,0:T(8,128)(2,1)}, bf16[2,128,2048]{2,1,0:T(8,128)(2,1)S(1)}, u32[]{:S(2)}, u32[]{:S(2)}) collective-permute-start(bf16[2,128,2048]{2,1,0:T(8,128)(2,1)} %bitcast.11), channel_id=1, source_target_pairs={{0,1},{1,0},{2,3},{3,2},{4,5},{5,4},{6,7},{7,6},{8,9},{9,8},{10,11... | collective-permute-start | bytes 3145736 | tf_op jit(solution)/shard_map/ppermute | solution.py:213
  0.5 1.3 %shard_map.64 = (bf16[2,128,2048]{2,1,0:T(8,128)(2,1)S(1)}, s32[8,128]{1,0:T(8,128)S(1)}, f32[4,256]{1,0:T(4,128)S(1)}, f32[4,256]{1,0:T(4,128)S(1)}, f32[4,256]{1,0:T(4,128)S(1)}, /*index=5*/f32[4,256]{1,0:T(4,128)S(1)}) custom-call(s32[8,256]{1,0:T(8,128)} %bitcast.13, bf16[8,256]{1,0:T(8,128)(2,1)} %bitcast.14, s32[8,8]{1,0:T(8,128)} %bitcast.15, ...), custom_call_target="tpu_custom_call" | custom-call | tf_op jit(solution)/shard_map/pallas_call | solution.py:216
  1.8 2.6 %collective-permute-start.1 = (f32[4,256]{1,0:T(4,128)S(1)}, f32[4,256]{1,0:T(4,128)S(1)}, u32[]{:S(2)}, u32[]{:S(2)}) collective-permute-start(f32[4,256]{1,0:T(4,128)S(1)} %get-tuple-element.18), channel_id=1, source_target_pairs={{0,2},{1,3},{2,0},{3,1},{4,6},{5,7},{6,4},{7,5},{8,10},{9,11},{10,... | collective-permute-start | bytes 12296 | tf_op jit(solution)/shard_map/ppermute | solution.py:230
  4.3 1.5 %collective-permute-start.3 = (f32[4,256]{1,0:T(4,128)S(1)}, f32[4,256]{1,0:T(4,128)S(1)}, u32[]{:S(2)}, u32[]{:S(2)}) collective-permute-start(f32[4,256]{1,0:T(4,128)S(1)} %get-tuple-element.19), channel_id=1, source_target_pairs={{0,4},{1,5},{2,6},{3,7},{4,0},{5,1},{6,2},{7,3},{8,12},{9,13},{10,... | collective-permute-start | bytes 12296 | tf_op jit(solution)/shard_map/ppermute | solution.py:230
  5.9 0.0 collective-permute-start.5
  5.9 0.0 collective-permute-done.1.wanted_ref
  5.9 0.0 collective-permute-done.other_ref
  5.9 0.2 shard_map.66
  6.1 2.1 %collective-permute-start.2 = (bf16[2,256,256]{2,1,0:T(8,128)(2,1)S(1)}, bf16[2,256,256]{2,1,0:T(8,128)(2,1)S(1)}, u32[]{:S(2)}, u32[]{:S(2)}) collective-permute-start(bf16[2,256,256]{2,1,0:T(8,128)(2,1)S(1)} %shard_map.66), channel_id=1, source_target_pairs={{0,2},{1,3},{2,0},{3,1},{4,6},{5,7},{6,4},{7,5},{8,10},{9,11},{10,... | collective-permute-start | bytes 786440 | tf_op jit(solution)/shard_map/ppermute | solution.py:253
  8.2 0.0 collective-permute-done.3.wanted_ref
  8.2 0.2 shard_map.68
  8.4 2.4 %collective-permute-start.4 = (bf16[2,256,256]{2,1,0:T(8,128)(2,1)S(1)}, bf16[2,256,256]{2,1,0:T(8,128)(2,1)S(1)}, u32[]{:S(2)}, u32[]{:S(2)}) collective-permute-start(bf16[2,256,256]{2,1,0:T(8,128)(2,1)S(1)} %shard_map.68), channel_id=1, source_target_pairs={{0,4},{1,5},{2,6},{3,7},{4,0},{5,1},{6,2},{7,3},{8,12},{9,13},{10,... | collective-permute-start | bytes 786440 | tf_op jit(solution)/shard_map/ppermute | solution.py:253
  10.8 0.0 collective-permute-done.5.wanted_ref
  10.8 1.0 %shard_map.69 = bf16[2,256,256]{2,1,0:T(8,128)(2,1)S(1)} custom-call(s32[8,128]{1,0:T(8,128)S(1)} %get-tuple-element.15.codes_ref, bf16[2,128,2048]{2,1,0:T(8,128)(2,1)S(1)} %get-tuple-element.16.own_ref, bf16[2,128,2048]{2,1,0:T(8,128)(2,1)S(1)} %collective-permute-done.other_ref, f32[4,256]{1,0:T(4,128)S(1)} %collective-permute-done.5.wanted_ref), custom_call_target="tpu_custom_call" | custom-call | flops 335544320 | bytes 4718592 | tf_op jit(solution)/shard_map/pallas_call | solution.py:235
  11.9 0.1 collective-permute-start.6
  12.0 0.0 copy-start
  12.0 0.2 shard_map.65.refs_0_
  12.2 3.2 %collective-permute-done.2.refs_1_ = bf16[2,256,256]{2,1,0:T(8,128)(2,1)S(1)} collective-permute-done((bf16[2,256,256]{2,1,0:T(8,128)(2,1)S(1)}, bf16[2,256,256]{2,1,0:T(8,128)(2,1)S(1)}, u32[]{:S(2)}, u32[]{:S(2)}) %collective-permute-start.2) | collective-permute-done | bytes 262176 | tf_op jit(solution)/shard_map/ppermute | solution.py:253
  15.4 0.0 copy-done
  15.4 0.4 %shard_map.67.before_ref = f32[2,256,384]{2,1,0:T(8,128)S(1)} custom-call(bf16[8,384,128]{2,1,0:T(8,128)(2,1)S(1)} %bitcast.9, bf16[2,256,256]{2,1,0:T(8,128)(2,1)S(1)} %shard_map.65.refs_0_, bf16[2,256,256]{2,1,0:T(8,128)(2,1)S(1)} %collective-permute-done.2.refs_1_), custom_call_target="tpu_custom_call" | custom-call | tf_op jit(solution)/shard_map/pallas_call | solution.py:260
  15.8 6.6 %collective-permute-done.4.refs_0_ = bf16[2,256,256]{2,1,0:T(8,128)(2,1)S(1)} collective-permute-done((bf16[2,256,256]{2,1,0:T(8,128)(2,1)S(1)}, bf16[2,256,256]{2,1,0:T(8,128)(2,1)S(1)}, u32[]{:S(2)}, u32[]{:S(2)}) %collective-permute-start.4) | collective-permute-done | bytes 262176 | tf_op jit(solution)/shard_map/ppermute | solution.py:253
  22.4 0.0 collective-permute-done.6.refs_1_
  22.4 0.5 %shard_map.70 = (f32[2,64,384]{2,1,0:T(8,128)S(1)}, bf16[2,64,384]{2,1,0:T(8,128)(2,1)S(1)}, bf16[2,64,384]{2,1,0:T(8,128)(2,1)S(1)}, bf16[2,64,384]{2,1,0:T(8,128)(2,1)S(1)}) custom-call(bf16[8,384,128]{2,1,0:T(8,128)(2,1)S(1)} %bitcast.10, f32[2,256,384]{2,1,0:T(8,128)S(1)} %shard_map.67.before_ref, ...), custom_call_target="tpu_custom_call" | custom-call | tf_op jit(solution)/shard_map/pallas_call | solution.py:267
  22.9 2.7 %collective-permute-start.7 = (bf16[2,64,384]{2,1,0:T(8,128)(2,1)S(1)}, bf16[2,64,384]{2,1,0:T(8,128)(2,1)S(1)}, u32[]{:S(2)}, u32[]{:S(2)}) collective-permute-start(bf16[2,64,384]{2,1,0:T(8,128)(2,1)S(1)} %get-tuple-element.22), channel_id=1, source_target_pairs={{0,16},{8,24},{16,0},{24,8},{1,17},{9,25},{17,1},{25,9},{2,18},{10... | collective-permute-start | bytes 294920 | tf_op jit(solution)/shard_map/ppermute | solution.py:277
  25.6 2.0 %collective-permute-start.8 = (bf16[2,64,384]{2,1,0:T(8,128)(2,1)S(1)}, bf16[2,64,384]{2,1,0:T(8,128)(2,1)S(1)}, u32[]{:S(2)}, u32[]{:S(2)}) collective-permute-start(bf16[2,64,384]{2,1,0:T(8,128)(2,1)S(1)} %get-tuple-element.23), channel_id=1, source_target_pairs={{0,24},{8,16},{16,8},{24,0},{1,25},{9,17},{17,9},{25,1},{2,26},{10... | collective-permute-start | bytes 294920 | tf_op jit(solution)/shard_map/ppermute | solution.py:277
  27.5 0.0 collective-permute-start.9
  27.6 5.9 %collective-permute-done.7.refs_1_ = bf16[2,64,384]{2,1,0:T(8,128)(2,1)S(1)} collective-permute-done((bf16[2,64,384]{2,1,0:T(8,128)(2,1)S(1)}, bf16[2,64,384]{2,1,0:T(8,128)(2,1)S(1)}, u32[]{:S(2)}, u32[]{:S(2)}) %collective-permute-start.7) | collective-permute-done | bytes 98336 | tf_op jit(solution)/shard_map/ppermute | solution.py:277
  33.4 0.1 shard_map.71.sums_ref
  33.5 0.0 collective-permute-done.8.refs_0_
  33.6 0.3 collective-permute-done.9.refs_1_
  33.8 0.8 %shard_map.72 = f32[64,384]{1,0:T(8,128)} custom-call(f32[3,64,384]{2,1,0:T(8,128)S(1)} %shard_map.71.sums_ref, bf16[2,64,384]{2,1,0:T(8,128)(2,1)S(1)} %collective-permute-done.8.refs_0_, bf16[2,64,384]{2,1,0:T(8,128)(2,1)S(1)} %collective-permute-done.9.refs_1_), custom_call_target="tpu_custom_call" | custom-call | tf_op jit(solution)/shard_map/pallas_call | solution.py:287
Async XLA Ops:
  0.0 5.9 %collective-permute-start = (bf16[2,128,2048]{2,1,0:T(8,128)(2,1)}, bf16[2,128,2048]{2,1,0:T(8,128)(2,1)S(1)}, u32[]{:S(2)}, u32[]{:S(2)}) collective-permute-start(bf16[2,128,2048]{2,1,0:T(8,128)(2,1)} %bitcast.11), channel_id=1, source_target_pairs={{0,1},{1,0},{2,3},{3,2},{4,5},{5,4},{6,7},{7,6},{8,9},{9,8},{10,11... | collective-permute-start | bytes 3145736 | tf_op jit(solution)/shard_map/ppermute | solution.py:213
  1.8 4.1 %collective-permute-start.1 = (f32[4,256]{1,0:T(4,128)S(1)}, f32[4,256]{1,0:T(4,128)S(1)}, u32[]{:S(2)}, u32[]{:S(2)}) collective-permute-start(f32[4,256]{1,0:T(4,128)S(1)} %get-tuple-element.18), channel_id=1, source_target_pairs={{0,2},{1,3},{2,0},{3,1},{4,6},{5,7},{6,4},{7,5},{8,10},{9,11},{10,... | collective-permute-start | bytes 12296 | tf_op jit(solution)/shard_map/ppermute | solution.py:230
  4.3 3.9 %collective-permute-start.3 = (f32[4,256]{1,0:T(4,128)S(1)}, f32[4,256]{1,0:T(4,128)S(1)}, u32[]{:S(2)}, u32[]{:S(2)}) collective-permute-start(f32[4,256]{1,0:T(4,128)S(1)} %get-tuple-element.19), channel_id=1, source_target_pairs={{0,4},{1,5},{2,6},{3,7},{4,0},{5,1},{6,2},{7,3},{8,12},{9,13},{10,... | collective-permute-start | bytes 12296 | tf_op jit(solution)/shard_map/ppermute | solution.py:230
  5.9 5.0 %collective-permute-start.5 = (f32[4,256]{1,0:T(4,128)S(1)}, f32[4,256]{1,0:T(4,128)S(1)}, u32[]{:S(2)}, u32[]{:S(2)}) collective-permute-start(f32[4,256]{1,0:T(4,128)S(1)} %get-tuple-element.20), channel_id=1, source_target_pairs={{0,6},{1,7},{2,4},{3,5},{4,2},{5,3},{6,0},{7,1},{8,14},{9,15},{10,... | collective-permute-start | bytes 12296 | tf_op jit(solution)/shard_map/ppermute | solution.py:230
  6.1 9.2 %collective-permute-start.2 = (bf16[2,256,256]{2,1,0:T(8,128)(2,1)S(1)}, bf16[2,256,256]{2,1,0:T(8,128)(2,1)S(1)}, u32[]{:S(2)}, u32[]{:S(2)}) collective-permute-start(bf16[2,256,256]{2,1,0:T(8,128)(2,1)S(1)} %shard_map.66), channel_id=1, source_target_pairs={{0,2},{1,3},{2,0},{3,1},{4,6},{5,7},{6,4},{7,5},{8,10},{9,11},{10,... | collective-permute-start | bytes 786440 | tf_op jit(solution)/shard_map/ppermute | solution.py:253
  8.4 14.0 %collective-permute-start.4 = (bf16[2,256,256]{2,1,0:T(8,128)(2,1)S(1)}, bf16[2,256,256]{2,1,0:T(8,128)(2,1)S(1)}, u32[]{:S(2)}, u32[]{:S(2)}) collective-permute-start(bf16[2,256,256]{2,1,0:T(8,128)(2,1)S(1)} %shard_map.68), channel_id=1, source_target_pairs={{0,4},{1,5},{2,6},{3,7},{4,0},{5,1},{6,2},{7,3},{8,12},{9,13},{10,... | collective-permute-start | bytes 786440 | tf_op jit(solution)/shard_map/ppermute | solution.py:253
  11.9 10.5 %collective-permute-start.6 = (bf16[2,256,256]{2,1,0:T(8,128)(2,1)S(1)}, bf16[2,256,256]{2,1,0:T(8,128)(2,1)S(1)}, u32[]{:S(2)}, u32[]{:S(2)}) collective-permute-start(bf16[2,256,256]{2,1,0:T(8,128)(2,1)S(1)} %shard_map.69), channel_id=1, source_target_pairs={{0,6},{1,7},{2,4},{3,5},{4,2},{5,3},{6,0},{7,1},{8,14},{9,15},{10,... | collective-permute-start | bytes 786440 | tf_op jit(solution)/shard_map/ppermute | solution.py:253
  12.0 3.4 %copy-start = (bf16[1,1,8,384,128]{4,3,2,1,0:T(8,128)(2,1)S(1)}, bf16[1,1,8,384,128]{4,3,2,1,0:T(8,128)(2,1)}, u32[]{:S(2)}) copy-start(bf16[1,1,8,384,128]{4,3,2,1,0:T(8,128)(2,1)} %param.11) | copy-start | bytes 2359300
  22.9 10.5 %collective-permute-start.7 = (bf16[2,64,384]{2,1,0:T(8,128)(2,1)S(1)}, bf16[2,64,384]{2,1,0:T(8,128)(2,1)S(1)}, u32[]{:S(2)}, u32[]{:S(2)}) collective-permute-start(bf16[2,64,384]{2,1,0:T(8,128)(2,1)S(1)} %get-tuple-element.22), channel_id=1, source_target_pairs={{0,16},{8,24},{16,0},{24,8},{1,17},{9,25},{17,1},{25,9},{2,18},{10... | collective-permute-start | bytes 294920 | tf_op jit(solution)/shard_map/ppermute | solution.py:277
  25.6 8.0 %collective-permute-start.8 = (bf16[2,64,384]{2,1,0:T(8,128)(2,1)S(1)}, bf16[2,64,384]{2,1,0:T(8,128)(2,1)S(1)}, u32[]{:S(2)}, u32[]{:S(2)}) collective-permute-start(bf16[2,64,384]{2,1,0:T(8,128)(2,1)S(1)} %get-tuple-element.23), channel_id=1, source_target_pairs={{0,24},{8,16},{16,8},{24,0},{1,25},{9,17},{17,9},{25,1},{2,26},{10... | collective-permute-start | bytes 294920 | tf_op jit(solution)/shard_map/ppermute | solution.py:277
  27.5 6.3 %collective-permute-start.9 = (bf16[2,64,384]{2,1,0:T(8,128)(2,1)S(1)}, bf16[2,64,384]{2,1,0:T(8,128)(2,1)S(1)}, u32[]{:S(2)}, u32[]{:S(2)}) collective-permute-start(bf16[2,64,384]{2,1,0:T(8,128)(2,1)S(1)} %get-tuple-element.24), channel_id=1, source_target_pairs={{0,8},{8,0},{16,24},{24,16},{1,9},{9,1},{17,25},{25,17},{2,10},{10... | collective-permute-start | bytes 294920 | tf_op jit(solution)/shard_map/ppermute | solution.py:277
where the time goes:
time: 34.9 us; the launch traced here: 34.6 us
  waiting for transfers between devices  16 us (46%)
  starting transfers between devices  13.8 us (40%)
  Pallas kernels  4.77 us (14%)
    ppermute x3, waiting for transfers between devices, local(): received.append(lax.ppermute(sent, 'tile', chip_pairs(step, tiles)))  9.8 us
    ppermute x3, waiting for transfers between devices, local(): summed.append(lax.ppermute(pieces[1 + place], 'shot', pairs(step, shots)))  6.15 us
    ppermute x3, starting transfers between devices, local(): summed.append(lax.ppermute(pieces[1 + place], 'shot', pairs(step, shots)))  4.62 us
    ppermute x3, starting transfers between devices, local(): received.append(lax.ppermute(sent, 'tile', chip_pairs(step, tiles)))  4.59 us
    ppermute x3, starting transfers between devices, local(): lax.ppermute(wanted[step], 'tile', chip_pairs(step, tiles))  4.09 us
    pallas_call x4, Pallas kernels, depth_traces(): pl.pallas_call(functools.partial(depth_kernel, step), out_shape=jax.Shape...  1.6 us
    pallas_call x1, Pallas kernels, local(): pl.pallas_call(functools.partial(wanted_kernel, tiles), out_shape=[jax.Sh...  1.33 us
    pallas_call x1, Pallas kernels, local(): pl.pallas_call(functools.partial(image_kernel, shots), out_shape=jax.Shap...  0.79 us
  transfers between devices with their start and end apart: 10, of which 4 were waited for; matrix products, arithmetic and copies ran while one was open for 0% of the time, Pallas kernels for 10%

commit v1 on v0

--- a/solution.py
+++ b/solution.py
@@ -135,7 +135,7 @@
             out_ref[other] = jnp.zeros(out_ref.shape[1:], out_ref.dtype)
 
 
-def add_chips(tiles, steps, amplitude_ref, depth_refs, total_ref, fresh):
+def add_chips(tiles, steps, amplitude_ref, depth_refs, total_ref, before_ref):
     receivers = amplitude_ref.shape[2]
     group = 4
     for base in range(0, len(steps), group):
@@ -152,13 +152,15 @@
                 axis=1,
             )
             added = lax.dot_general(traces, weights, NT_DIMS, preferred_element_type=jnp.float32)
-            if base or not fresh:
+            if base:
                 added = added + total_ref[part]
+            elif before_ref is not None:
+                added = added + before_ref[part]
             total_ref[part] = added
 
 
 def gather_kernel(tiles, steps, amplitude_ref, *refs):
-    add_chips(tiles, steps, amplitude_ref, refs[:-1], refs[-1], True)
+    add_chips(tiles, steps, amplitude_ref, refs[:-1], refs[-1], None)
 
 
 def partial_kernel(tiles, shots, steps, amplitude_ref, before_ref, *refs):
@@ -166,8 +168,7 @@
     depth_refs = refs[: len(steps)]
     own_ref, out_refs, total_ref = refs[len(steps)], refs[len(steps) + 1 : -1], refs[-1]
     span = own_ref.shape[1]
-    total_ref[...] = before_ref[...]
-    add_chips(tiles, steps, amplitude_ref, depth_refs, total_ref, False)
+    add_chips(tiles, steps, amplitude_ref, depth_refs, total_ref, before_ref)
     for part in range(2):
         own_ref[part] = total_ref[part, pl.ds(pl.multiple_of(my_shot * span, span), span), :]
         for place, step in enumerate(steps_of(shots)):

time: 34.9 us -> 34.1 us (0.977)
  starting transfers between devices: 13.8 us -> 12.9 us
  Pallas kernels: 4.77 us -> 5.19 us
  waiting for transfers between devices: 16 us -> 15.6 us
    ppermute x3, starting transfers between devices: 4.59 us -> 3.73 us  [local(): received.append(lax.ppermute(sent, 'tile', chip_pairs(step, tiles)))]
    ppermute x3, waiting for transfers between devices: 6.15 us -> 5.49 us  [local(): summed.append(lax.ppermute(pieces[1 + place], 'shot', pairs(step, shots)))]
    pallas_call x4, Pallas kernels: 1.6 us -> 2.02 us  [depth_traces(): pl.pallas_call(functools.partial(depth_kernel, step), out_shape=jax.Shape...]
  transfers between devices with their start and end apart: 10 -> 10, of which waited for: 4 -> 4; matrix products, arithmetic and copies ran while one was open for 0% -> 0% of each run, Pallas kernels for 10% -> 12%
where the time goes in v1:
time: 34.1 us; the launch traced here: 33.8 us
  waiting for transfers between devices  15.6 us (46%)
  starting transfers between devices  12.9 us (38%)
  Pallas kernels  5.19 us (15%)
    ppermute x3, waiting for transfers between devices, local(): received.append(lax.ppermute(sent, 'tile', chip_pairs(step, tiles)))  10 us
    ppermute x3, waiting for transfers between devices, local(): summed.append(lax.ppermute(pieces[1 + place], 'shot', pairs(step, shots)))  5.49 us
    ppermute x3, starting transfers between devices, local(): summed.append(lax.ppermute(pieces[1 + place], 'shot', pairs(step, shots)))  4.66 us
    ppermute x3, starting transfers between devices, local(): lax.ppermute(wanted[step], 'tile', chip_pairs(step, tiles))  4.09 us
    ppermute x3, starting transfers between devices, local(): received.append(lax.ppermute(sent, 'tile', chip_pairs(step, tiles)))  3.73 us
    pallas_call x4, Pallas kernels, depth_traces(): pl.pallas_call(functools.partial(depth_kernel, step), out_shape=jax.Shape...  2.02 us
    pallas_call x1, Pallas kernels, local(): pl.pallas_call(functools.partial(wanted_kernel, tiles), out_shape=[jax.Sh...  1.33 us
    pallas_call x1, Pallas kernels, local(): pl.pallas_call(functools.partial(image_kernel, shots), out_shape=jax.Shap...  0.79 us
  transfers between devices with their start and end apart: 10, of which 4 were waited for; matrix products, arithmetic and copies ran while one was open for 0% of the time, Pallas kernels for 12%

profile of v1, /device:TPU:0, one launch (start us, length us, event | category | flops | bytes accessed | tf_op | source)
XLA Modules:
  0.0 33.8 jit_solution(5425444367590659903)
XLA Ops:
  0.0 0.5 %collective-permute-start = (bf16[2,128,2048]{2,1,0:T(8,128)(2,1)}, bf16[2,128,2048]{2,1,0:T(8,128)(2,1)S(1)}, u32[]{:S(2)}, u32[]{:S(2)}) collective-permute-start(bf16[2,128,2048]{2,1,0:T(8,128)(2,1)} %bitcast.11), channel_id=1, source_target_pairs={{0,1},{1,0},{2,3},{3,2},{4,5},{5,4},{6,7},{7,6},{8,9},{9,8},{10,11... | collective-permute-start | bytes 3145736 | tf_op jit(solution)/shard_map/ppermute | solution.py:214
  0.5 1.3 %shard_map.64 = (bf16[2,128,2048]{2,1,0:T(8,128)(2,1)S(1)}, s32[8,128]{1,0:T(8,128)S(1)}, f32[4,256]{1,0:T(4,128)S(1)}, f32[4,256]{1,0:T(4,128)S(1)}, f32[4,256]{1,0:T(4,128)S(1)}, /*index=5*/f32[4,256]{1,0:T(4,128)S(1)}) custom-call(s32[8,256]{1,0:T(8,128)} %bitcast.13, bf16[8,256]{1,0:T(8,128)(2,1)} %bitcast.14, s32[8,8]{1,0:T(8,128)} %bitcast.15, ...), custom_call_target="tpu_custom_call" | custom-call | tf_op jit(solution)/shard_map/pallas_call | solution.py:217
  1.8 2.6 %collective-permute-start.1 = (f32[4,256]{1,0:T(4,128)S(1)}, f32[4,256]{1,0:T(4,128)S(1)}, u32[]{:S(2)}, u32[]{:S(2)}) collective-permute-start(f32[4,256]{1,0:T(4,128)S(1)} %get-tuple-element.18), channel_id=1, source_target_pairs={{0,2},{1,3},{2,0},{3,1},{4,6},{5,7},{6,4},{7,5},{8,10},{9,11},{10,... | collective-permute-start | bytes 12296 | tf_op jit(solution)/shard_map/ppermute | solution.py:231
  4.3 1.5 %collective-permute-start.3 = (f32[4,256]{1,0:T(4,128)S(1)}, f32[4,256]{1,0:T(4,128)S(1)}, u32[]{:S(2)}, u32[]{:S(2)}) collective-permute-start(f32[4,256]{1,0:T(4,128)S(1)} %get-tuple-element.19), channel_id=1, source_target_pairs={{0,4},{1,5},{2,6},{3,7},{4,0},{5,1},{6,2},{7,3},{8,12},{9,13},{10,... | collective-permute-start | bytes 12296 | tf_op jit(solution)/shard_map/ppermute | solution.py:231
  5.9 0.0 collective-permute-start.5
  5.9 0.0 collective-permute-done.1.wanted_ref
  5.9 0.0 collective-permute-done.other_ref
  5.9 1.0 %shard_map.66 = bf16[2,256,256]{2,1,0:T(8,128)(2,1)S(1)} custom-call(s32[8,128]{1,0:T(8,128)S(1)} %get-tuple-element.15.codes_ref, bf16[2,128,2048]{2,1,0:T(8,128)(2,1)S(1)} %get-tuple-element.16.own_ref, bf16[2,128,2048]{2,1,0:T(8,128)(2,1)S(1)} %collective-permute-done.other_ref, f32[4,256]{1,0:T(4,128)S(1)} %collective-permute-done.1.wanted_ref), custom_call_target="tpu_custom_call" | custom-call | flops 335544320 | bytes 4718592 | tf_op jit(solution)/shard_map/pallas_call | solution.py:236
  7.0 2.1 %collective-permute-start.2 = (bf16[2,256,256]{2,1,0:T(8,128)(2,1)S(1)}, bf16[2,256,256]{2,1,0:T(8,128)(2,1)S(1)}, u32[]{:S(2)}, u32[]{:S(2)}) collective-permute-start(bf16[2,256,256]{2,1,0:T(8,128)(2,1)S(1)} %shard_map.66), channel_id=1, source_target_pairs={{0,2},{1,3},{2,0},{3,1},{4,6},{5,7},{6,4},{7,5},{8,10},{9,11},{10,... | collective-permute-start | bytes 786440 | tf_op jit(solution)/shard_map/ppermute | solution.py:254
  9.1 0.0 collective-permute-done.3.wanted_ref
  9.1 0.2 shard_map.68
  9.3 1.2 %collective-permute-start.4 = (bf16[2,256,256]{2,1,0:T(8,128)(2,1)S(1)}, bf16[2,256,256]{2,1,0:T(8,128)(2,1)S(1)}, u32[]{:S(2)}, u32[]{:S(2)}) collective-permute-start(bf16[2,256,256]{2,1,0:T(8,128)(2,1)S(1)} %shard_map.68), channel_id=1, source_target_pairs={{0,4},{1,5},{2,6},{3,7},{4,0},{5,1},{6,2},{7,3},{8,12},{9,13},{10,... | collective-permute-start | bytes 786440 | tf_op jit(solution)/shard_map/ppermute | solution.py:254
  10.4 0.0 collective-permute-done.5.wanted_ref
  10.4 0.2 shard_map.69
  10.6 0.5 %collective-permute-start.6 = (bf16[2,256,256]{2,1,0:T(8,128)(2,1)S(1)}, bf16[2,256,256]{2,1,0:T(8,128)(2,1)S(1)}, u32[]{:S(2)}, u32[]{:S(2)}) collective-permute-start(bf16[2,256,256]{2,1,0:T(8,128)(2,1)S(1)} %shard_map.69), channel_id=1, source_target_pairs={{0,6},{1,7},{2,4},{3,5},{4,2},{5,3},{6,0},{7,1},{8,14},{9,15},{10,... | collective-permute-start | bytes 786440 | tf_op jit(solution)/shard_map/ppermute | solution.py:254
  11.1 0.0 copy-start
  11.1 0.6 %shard_map.65.refs_0_ = bf16[2,256,256]{2,1,0:T(8,128)(2,1)S(1)} custom-call(s32[8,128]{1,0:T(8,128)S(1)} %get-tuple-element.15.codes_ref, bf16[2,128,2048]{2,1,0:T(8,128)(2,1)S(1)} %get-tuple-element.16.own_ref, bf16[2,128,2048]{2,1,0:T(8,128)(2,1)S(1)} %collective-permute-done.other_ref, f32[4,256]{1,0:T(4,128)S(1)} %get-tuple-element.17.wanted_ref), custom_call_target="tpu_custom_call" | custom-call | flops 335544320 | bytes 4718592 | tf_op jit(solution)/shard_map/pallas_call | solution.py:236
  11.7 4.5 %collective-permute-done.2.refs_1_ = bf16[2,256,256]{2,1,0:T(8,128)(2,1)S(1)} collective-permute-done((bf16[2,256,256]{2,1,0:T(8,128)(2,1)S(1)}, bf16[2,256,256]{2,1,0:T(8,128)(2,1)S(1)}, u32[]{:S(2)}, u32[]{:S(2)}) %collective-permute-start.2) | collective-permute-done | bytes 262176 | tf_op jit(solution)/shard_map/ppermute | solution.py:254
  16.3 0.0 copy-done
  16.3 0.4 %shard_map.67.before_ref = f32[2,256,384]{2,1,0:T(8,128)S(1)} custom-call(bf16[8,384,128]{2,1,0:T(8,128)(2,1)S(1)} %bitcast.9, bf16[2,256,256]{2,1,0:T(8,128)(2,1)S(1)} %shard_map.65.refs_0_, bf16[2,256,256]{2,1,0:T(8,128)(2,1)S(1)} %collective-permute-done.2.refs_1_), custom_call_target="tpu_custom_call" | custom-call | tf_op jit(solution)/shard_map/pallas_call | solution.py:261
  16.7 5.5 %collective-permute-done.4.refs_0_ = bf16[2,256,256]{2,1,0:T(8,128)(2,1)S(1)} collective-permute-done((bf16[2,256,256]{2,1,0:T(8,128)(2,1)S(1)}, bf16[2,256,256]{2,1,0:T(8,128)(2,1)S(1)}, u32[]{:S(2)}, u32[]{:S(2)}) %collective-permute-start.4) | collective-permute-done | bytes 262176 | tf_op jit(solution)/shard_map/ppermute | solution.py:254
  22.2 0.0 collective-permute-done.6.refs_1_
  22.2 0.5 %shard_map.70 = (f32[2,64,384]{2,1,0:T(8,128)S(1)}, bf16[2,64,384]{2,1,0:T(8,128)(2,1)S(1)}, bf16[2,64,384]{2,1,0:T(8,128)(2,1)S(1)}, bf16[2,64,384]{2,1,0:T(8,128)(2,1)S(1)}) custom-call(bf16[8,384,128]{2,1,0:T(8,128)(2,1)S(1)} %bitcast.10, f32[2,256,384]{2,1,0:T(8,128)S(1)} %shard_map.67.before_ref, ...), custom_call_target="tpu_custom_call" | custom-call | tf_op jit(solution)/shard_map/pallas_call | solution.py:268
  22.7 2.7 %collective-permute-start.7 = (bf16[2,64,384]{2,1,0:T(8,128)(2,1)S(1)}, bf16[2,64,384]{2,1,0:T(8,128)(2,1)S(1)}, u32[]{:S(2)}, u32[]{:S(2)}) collective-permute-start(bf16[2,64,384]{2,1,0:T(8,128)(2,1)S(1)} %get-tuple-element.22), channel_id=1, source_target_pairs={{0,16},{8,24},{16,0},{24,8},{1,17},{9,25},{17,1},{25,9},{2,18},{10... | collective-permute-start | bytes 294920 | tf_op jit(solution)/shard_map/ppermute | solution.py:278
  25.4 1.6 %collective-permute-start.8 = (bf16[2,64,384]{2,1,0:T(8,128)(2,1)S(1)}, bf16[2,64,384]{2,1,0:T(8,128)(2,1)S(1)}, u32[]{:S(2)}, u32[]{:S(2)}) collective-permute-start(bf16[2,64,384]{2,1,0:T(8,128)(2,1)S(1)} %get-tuple-element.23), channel_id=1, source_target_pairs={{0,24},{8,16},{16,8},{24,0},{1,25},{9,17},{17,9},{25,1},{2,26},{10... | collective-permute-start | bytes 294920 | tf_op jit(solution)/shard_map/ppermute | solution.py:278
  26.9 0.4 %collective-permute-start.9 = (bf16[2,64,384]{2,1,0:T(8,128)(2,1)S(1)}, bf16[2,64,384]{2,1,0:T(8,128)(2,1)S(1)}, u32[]{:S(2)}, u32[]{:S(2)}) collective-permute-start(bf16[2,64,384]{2,1,0:T(8,128)(2,1)S(1)} %get-tuple-element.24), channel_id=1, source_target_pairs={{0,8},{8,0},{16,24},{24,16},{1,9},{9,1},{17,25},{25,17},{2,10},{10... | collective-permute-start | bytes 294920 | tf_op jit(solution)/shard_map/ppermute | solution.py:278
  27.4 5.0 %collective-permute-done.7.refs_1_ = bf16[2,64,384]{2,1,0:T(8,128)(2,1)S(1)} collective-permute-done((bf16[2,64,384]{2,1,0:T(8,128)(2,1)S(1)}, bf16[2,64,384]{2,1,0:T(8,128)(2,1)S(1)}, u32[]{:S(2)}, u32[]{:S(2)}) %collective-permute-start.7) | collective-permute-done | bytes 98336 | tf_op jit(solution)/shard_map/ppermute | solution.py:278
  32.3 0.1 shard_map.71.sums_ref
  32.5 0.0 collective-permute-done.8.refs_0_
  32.5 0.5 %collective-permute-done.9.refs_1_ = bf16[2,64,384]{2,1,0:T(8,128)(2,1)S(1)} collective-permute-done((bf16[2,64,384]{2,1,0:T(8,128)(2,1)S(1)}, bf16[2,64,384]{2,1,0:T(8,128)(2,1)S(1)}, u32[]{:S(2)}, u32[]{:S(2)}) %collective-permute-start.9) | collective-permute-done | bytes 98336 | tf_op jit(solution)/shard_map/ppermute | solution.py:278
  33.0 0.8 %shard_map.72 = f32[64,384]{1,0:T(8,128)} custom-call(f32[3,64,384]{2,1,0:T(8,128)S(1)} %shard_map.71.sums_ref, bf16[2,64,384]{2,1,0:T(8,128)(2,1)S(1)} %collective-permute-done.8.refs_0_, bf16[2,64,384]{2,1,0:T(8,128)(2,1)S(1)} %collective-permute-done.9.refs_1_), custom_call_target="tpu_custom_call" | custom-call | tf_op jit(solution)/shard_map/pallas_call | solution.py:288
Async XLA Ops:
  0.0 5.9 %collective-permute-start = (bf16[2,128,2048]{2,1,0:T(8,128)(2,1)}, bf16[2,128,2048]{2,1,0:T(8,128)(2,1)S(1)}, u32[]{:S(2)}, u32[]{:S(2)}) collective-permute-start(bf16[2,128,2048]{2,1,0:T(8,128)(2,1)} %bitcast.11), channel_id=1, source_target_pairs={{0,1},{1,0},{2,3},{3,2},{4,5},{5,4},{6,7},{7,6},{8,9},{9,8},{10,11... | collective-permute-start | bytes 3145736 | tf_op jit(solution)/shard_map/ppermute | solution.py:214
  1.8 4.1 %collective-permute-start.1 = (f32[4,256]{1,0:T(4,128)S(1)}, f32[4,256]{1,0:T(4,128)S(1)}, u32[]{:S(2)}, u32[]{:S(2)}) collective-permute-start(f32[4,256]{1,0:T(4,128)S(1)} %get-tuple-element.18), channel_id=1, source_target_pairs={{0,2},{1,3},{2,0},{3,1},{4,6},{5,7},{6,4},{7,5},{8,10},{9,11},{10,... | collective-permute-start | bytes 12296 | tf_op jit(solution)/shard_map/ppermute | solution.py:231
  4.3 4.7 %collective-permute-start.3 = (f32[4,256]{1,0:T(4,128)S(1)}, f32[4,256]{1,0:T(4,128)S(1)}, u32[]{:S(2)}, u32[]{:S(2)}) collective-permute-start(f32[4,256]{1,0:T(4,128)S(1)} %get-tuple-element.19), channel_id=1, source_target_pairs={{0,4},{1,5},{2,6},{3,7},{4,0},{5,1},{6,2},{7,3},{8,12},{9,13},{10,... | collective-permute-start | bytes 12296 | tf_op jit(solution)/shard_map/ppermute | solution.py:231
  5.9 4.6 %collective-permute-start.5 = (f32[4,256]{1,0:T(4,128)S(1)}, f32[4,256]{1,0:T(4,128)S(1)}, u32[]{:S(2)}, u32[]{:S(2)}) collective-permute-start(f32[4,256]{1,0:T(4,128)S(1)} %get-tuple-element.20), channel_id=1, source_target_pairs={{0,6},{1,7},{2,4},{3,5},{4,2},{5,3},{6,0},{7,1},{8,14},{9,15},{10,... | collective-permute-start | bytes 12296 | tf_op jit(solution)/shard_map/ppermute | solution.py:231
  7.0 9.3 %collective-permute-start.2 = (bf16[2,256,256]{2,1,0:T(8,128)(2,1)S(1)}, bf16[2,256,256]{2,1,0:T(8,128)(2,1)S(1)}, u32[]{:S(2)}, u32[]{:S(2)}) collective-permute-start(bf16[2,256,256]{2,1,0:T(8,128)(2,1)S(1)} %shard_map.66), channel_id=1, source_target_pairs={{0,2},{1,3},{2,0},{3,1},{4,6},{5,7},{6,4},{7,5},{8,10},{9,11},{10,... | collective-permute-start | bytes 786440 | tf_op jit(solution)/shard_map/ppermute | solution.py:254
  9.3 12.9 %collective-permute-start.4 = (bf16[2,256,256]{2,1,0:T(8,128)(2,1)S(1)}, bf16[2,256,256]{2,1,0:T(8,128)(2,1)S(1)}, u32[]{:S(2)}, u32[]{:S(2)}) collective-permute-start(bf16[2,256,256]{2,1,0:T(8,128)(2,1)S(1)} %shard_map.68), channel_id=1, source_target_pairs={{0,4},{1,5},{2,6},{3,7},{4,0},{5,1},{6,2},{7,3},{8,12},{9,13},{10,... | collective-permute-start | bytes 786440 | tf_op jit(solution)/shard_map/ppermute | solution.py:254
  10.6 11.6 %collective-permute-start.6 = (bf16[2,256,256]{2,1,0:T(8,128)(2,1)S(1)}, bf16[2,256,256]{2,1,0:T(8,128)(2,1)S(1)}, u32[]{:S(2)}, u32[]{:S(2)}) collective-permute-start(bf16[2,256,256]{2,1,0:T(8,128)(2,1)S(1)} %shard_map.69), channel_id=1, source_target_pairs={{0,6},{1,7},{2,4},{3,5},{4,2},{5,3},{6,0},{7,1},{8,14},{9,15},{10,... | collective-permute-start | bytes 786440 | tf_op jit(solution)/shard_map/ppermute | solution.py:254
  11.1 5.2 %copy-start = (bf16[1,1,8,384,128]{4,3,2,1,0:T(8,128)(2,1)S(1)}, bf16[1,1,8,384,128]{4,3,2,1,0:T(8,128)(2,1)}, u32[]{:S(2)}) copy-start(bf16[1,1,8,384,128]{4,3,2,1,0:T(8,128)(2,1)} %param.11) | copy-start | bytes 2359300
  22.7 9.6 %collective-permute-start.7 = (bf16[2,64,384]{2,1,0:T(8,128)(2,1)S(1)}, bf16[2,64,384]{2,1,0:T(8,128)(2,1)S(1)}, u32[]{:S(2)}, u32[]{:S(2)}) collective-permute-start(bf16[2,64,384]{2,1,0:T(8,128)(2,1)S(1)} %get-tuple-element.22), channel_id=1, source_target_pairs={{0,16},{8,24},{16,0},{24,8},{1,17},{9,25},{17,1},{25,9},{2,18},{10... | collective-permute-start | bytes 294920 | tf_op jit(solution)/shard_map/ppermute | solution.py:278
  25.4 7.1 %collective-permute-start.8 = (bf16[2,64,384]{2,1,0:T(8,128)(2,1)S(1)}, bf16[2,64,384]{2,1,0:T(8,128)(2,1)S(1)}, u32[]{:S(2)}, u32[]{:S(2)}) collective-permute-start(bf16[2,64,384]{2,1,0:T(8,128)(2,1)S(1)} %get-tuple-element.23), channel_id=1, source_target_pairs={{0,24},{8,16},{16,8},{24,0},{1,25},{9,17},{17,9},{25,1},{2,26},{10... | collective-permute-start | bytes 294920 | tf_op jit(solution)/shard_map/ppermute | solution.py:278
  26.9 6.1 %collective-permute-start.9 = (bf16[2,64,384]{2,1,0:T(8,128)(2,1)S(1)}, bf16[2,64,384]{2,1,0:T(8,128)(2,1)S(1)}, u32[]{:S(2)}, u32[]{:S(2)}) collective-permute-start(bf16[2,64,384]{2,1,0:T(8,128)(2,1)S(1)} %get-tuple-element.24), channel_id=1, source_target_pairs={{0,8},{8,0},{16,24},{24,16},{1,9},{9,1},{17,25},{25,17},{2,10},{10... | collective-permute-start | bytes 294920 | tf_op jit(solution)/shard_map/ppermute | solution.py:278
